TPU v7x, 32 devices: a whole 2x2x4 slice. The times are simulated.
32 devices in a mesh: row: 8 (over z, core), col: 4 (over y, x).
Axes of the slice: x: 2, y: 2, z: 4, core: 2. Of those that a mesh axis runs over, the one named last changes fastest.
Arguments:
- shot_traces: float32 [16384, 2, 8192], P(('row', 'col')), may hold values from -0.046875 to 0.046875
- shot_ids: int32 [16384], P(('row', 'col')), may hold values from 0 to 8191, as said below
- shot_counts: int32 [32], P(('row', 'col')), may hold values from 0 to 512, as said below
- missing_blocks: int32 [64, 64], P('row', 'col'), may hold values from 0 to 1, as said below
- weight_bins: int32 [8192], P(('row', 'col')), may hold values from 0 to 63
- weight_table: float32 [64], replicated, may hold values from 0.1 to 1
- focus_panel: float32 [2, 8192, 512], P(None, ('col', 'row')), may hold values from -6 to 6
Outputs:
- wavefield: float32 [2, 8192, 512], P(None, ('row', 'col'))
- adjoint_image: float32 [2, 8192, 512], P(None, ('col', 'row'))
Inputs may be any that keep to these rules, and one draw needn't show every extreme that they name: `shot_ids`: over the counted slots of all devices every source appears exactly once; uncounted slots hold arbitrary sources. The counted slots of one device hold at most 64 sources of any block of 1024 consecutive sources, and at most (128) of any block of 2048; some device reaches both. `shot_counts`: some device has all 512 slots counted. `missing_blocks`: diagonal blocks are recorded, and of two mirrored blocks at most one is missing.
All inputs are finite; a program needn't handle non-finite values.
Results may differ from a plain program's by a relative error of at most 0.00007.
Values sent between devices are 32-bit elements; how exact they have to be, the bound alone decides.
A program may use at most 320 MiB of HBM per device.

v0:
```python
import jax
import jax.numpy as jnp
from jax import lax
from jax.sharding import PartitionSpec as P


def high_dot(left, right):
    return jnp.dot(left, right, precision=lax.Precision.HIGHEST, preferred_element_type=jnp.float32)


def trans_dot(left, right):
    return lax.dot_general(
        left,
        right,
        (((0,), (0,)), ((), ())),
        precision=lax.Precision.HIGHEST,
        preferred_element_type=jnp.float32,
    )


def pack_slots(traces, labels, held_count, group_size, group_count, capacity):
    slot_total = labels.shape[0]
    slot_index = jnp.arange(slot_total, dtype=jnp.int32)
    is_used = slot_index < held_count
    dest_group = labels // group_size
    onehot = (
        (dest_group[:, None] == jnp.arange(group_count, dtype=jnp.int32)[None, :])
        & is_used[:, None]
    ).astype(jnp.int32)
    before = jnp.cumsum(onehot, axis=0) - onehot
    rank_in = jnp.sum(before * onehot, axis=1)
    position = jnp.where(is_used, dest_group * capacity + rank_in, group_count * capacity)
    source = (
        jnp.full((group_count * capacity,), slot_total, jnp.int32)
        .at[position]
        .set(slot_index, mode="drop")
    )
    packed = jnp.take(traces, source, axis=0, mode="fill", fill_value=0.0)
    packed_labels = jnp.take(labels, source, axis=0, mode="fill", fill_value=-1)
    return (packed, packed_labels)


def place_rows(arrived, labels, first_label, length):
    has_label = labels >= 0
    target = jnp.where(has_label, labels - first_label, length)
    source = (
        jnp.zeros((length,), jnp.int32)
        .at[target]
        .set(jnp.arange(labels.shape[0], dtype=jnp.int32), mode="drop")
    )
    return jnp.take(arrived, source, axis=0)


def lookup(bins, table):
    matches = bins[:, None] == jnp.arange(table.shape[0], dtype=jnp.int32)[None, :]
    return jnp.sum(jnp.where(matches, table[None, :], 0.0), axis=1)


def local(
    shot_traces, shot_ids, shot_counts, missing_blocks, weight_bins, weight_table, focus_panel
):
    slot_total = shot_traces.shape[0]
    stations = shot_traces.shape[2]
    row_count = lax.axis_size("row")
    col_count = lax.axis_size("col")
    src_tile = stations // row_count
    rcv_tile = stations // col_count
    row_index = lax.axis_index("row")
    col_index = lax.axis_index("col")
    held_count = shot_counts[0]
    packed, packed_labels = pack_slots(
        shot_traces, shot_ids, held_count, src_tile, row_count, slot_total // row_count
    )
    outgoing = packed.reshape(slot_total, 2, col_count, rcv_tile)
    label_copies = jnp.broadcast_to(packed_labels[:, None, None], (slot_total, 1, col_count))
    arrived, arrived_labels = (
        lax.all_to_all(
            lax.all_to_all(outgoing, "row", split_axis=0, concat_axis=0, tiled=True),
            "col",
            split_axis=2,
            concat_axis=0,
            tiled=True,
        ),
        lax.all_to_all(
            lax.all_to_all(label_copies, "row", split_axis=0, concat_axis=0, tiled=True),
            "col",
            split_axis=2,
            concat_axis=0,
            tiled=True,
        ),
    )
    direct = place_rows(
        arrived.reshape(-1, 2, rcv_tile), arrived_labels.reshape(-1), row_index * src_tile, src_tile
    )
    capacity_rec = slot_total // col_count
    packed_mirror, mirror_labels = pack_slots(
        shot_traces, shot_ids, held_count, rcv_tile, col_count, capacity_rec
    )
    mirror_out = packed_mirror.reshape(slot_total, 2, row_count, src_tile)
    mirror_copies = jnp.broadcast_to(mirror_labels[:, None, None], (slot_total, 1, row_count))
    halfway, halfway_labels = (
        lax.all_to_all(mirror_out, "row", split_axis=2, concat_axis=0, tiled=True),
        lax.all_to_all(mirror_copies, "row", split_axis=2, concat_axis=0, tiled=True),
    )
    halfway = halfway.reshape(row_count, col_count, capacity_rec, 2, src_tile)
    halfway_labels = halfway_labels.reshape(row_count, col_count, capacity_rec)
    mirrored, mirrored_labels = (
        lax.all_to_all(halfway, "col", split_axis=1, concat_axis=0, tiled=True),
        lax.all_to_all(halfway_labels, "col", split_axis=1, concat_axis=0, tiled=True),
    )
    transposed = place_rows(
        mirrored.reshape(-1, 2, src_tile),
        mirrored_labels.reshape(-1),
        col_index * rcv_tile,
        rcv_tile,
    )
    blocks_down = missing_blocks.shape[0]
    blocks_across = missing_blocks.shape[1]
    block_size = src_tile // blocks_down
    is_missing = jnp.broadcast_to(
        missing_blocks[:, None, :, None] > 0, (blocks_down, block_size, blocks_across, block_size)
    ).reshape(src_tile, rcv_tile)
    kernel_re = jnp.where(is_missing, transposed[:, 0, :].T, direct[:, 0, :])
    kernel_im = jnp.where(is_missing, transposed[:, 1, :].T, direct[:, 1, :])
    focus_all = lax.all_gather(focus_panel, "row", axis=1, tiled=True)
    panel_re = focus_all[0]
    panel_im = focus_all[1]
    field_re = high_dot(kernel_re, panel_re) - high_dot(kernel_im, panel_im)
    field_im = high_dot(kernel_re, panel_im) + high_dot(kernel_im, panel_re)
    own_rows = lax.psum_scatter(
        jnp.stack([field_re, field_im], axis=1), "col", scatter_dimension=0, tiled=True
    )
    weighted = own_rows * lookup(weight_bins, weight_table)[:, None, None]
    weighted_all = lax.all_gather(weighted, "col", axis=0, tiled=True)
    weighted_re = weighted_all[:, 0, :]
    weighted_im = weighted_all[:, 1, :]
    image_re = trans_dot(kernel_re, weighted_re) + trans_dot(kernel_im, weighted_im)
    image_im = trans_dot(kernel_re, weighted_im) - trans_dot(kernel_im, weighted_re)
    image_rows = lax.psum_scatter(
        jnp.stack([image_re, image_im], axis=1), "row", scatter_dimension=0, tiled=True
    )
    return (jnp.swapaxes(own_rows, 0, 1), jnp.swapaxes(image_rows, 0, 1))


def solution(mesh):
    placed = (
        P(("row", "col"), None, None),
        P(("row", "col")),
        P(("row", "col")),
        P("row", "col"),
        P(("row", "col")),
        P(),
        P(None, ("col", "row"), None),
    )
    return jax.shard_map(
        local,
        mesh=mesh,
        in_specs=placed,
        out_specs=(P(None, ("row", "col"), None), P(None, ("col", "row"), None)),
        check_vma=False,
    )
```

profile of v0, /device:TPU:0, one launch (start us, length us, event | category | flops | bytes accessed | tf_op | source)
XLA Modules:
  0.0 3004.8 jit_solution(7320027503806781261)
XLA Ops:
  22.1 6.4 all-to-all-start.4
  35.1 5.1 all-to-all-start
  49.6 45.2 %gather_fusion.3 = f32[512,2,8192]{2,1,0:T(2,128)} fusion(f32[512,2,8192]{2,1,0:T(2,128)} %param.11, s32[1024]{0:T(1024)S(1)} %pad_clamp_fusion.1), kind=kCustom, calls=%fused_computation.1.clone | custom fusion | bytes 67110912 | tf_op jit(solution)/shard_map/jit(_take)/gather | solution.py:38
  96.1 4.1 all-to-all-start.1
  100.2 24.2 broadcast_select_fusion.1
  124.4 48.8 %copy.56 = f32[512,2,8192]{0,2,1:T(8,128)} copy(f32[512,2,8192]{2,1,0:T(2,128)} %broadcast_select_fusion.1) | data formatting | bytes 67108864 | tf_op jit(solution)/shard_map/jit(_take)/select_n | solution.py:38
  173.1 22.9 copy.57
  196.6 7.3 all-to-all-start.2
  203.9 46.5 %gather_fusion.5 = f32[512,2,8192]{2,1,0:T(2,128)} fusion(f32[512,2,8192]{2,1,0:T(2,128)} %param.11, s32[1024]{0:T(1024)S(1)} %pad_clamp_fusion), kind=kCustom, calls=%fused_computation.3.clone | custom fusion | bytes 67110912 | tf_op jit(solution)/shard_map/jit(_take)/gather | solution.py:38
  250.5 24.2 broadcast_select_fusion
  274.6 48.7 %copy.64 = f32[512,2,8192]{0,2,1:T(8,128)} copy(f32[512,2,8192]{2,1,0:T(2,128)} %broadcast_select_fusion) | data formatting | bytes 67108864 | tf_op jit(solution)/shard_map/jit(_take)/select_n | solution.py:38
  323.4 39.8 %copy.65 = f32[512,2,4,2048]{3,2,1,0:T(4,128)} copy(f32[512,2,4,2048]{0,3,2,1:T(8,128)} %bitcast.133) | data formatting | bytes 67108864 | tf_op jit(solution)/shard_map/reshape | solution.py:74
  363.2 563.9 %all-to-all-done.2 = f32[512,2,8,1024]{0,3,1,2:T(8,128)} async-done(((f32[512,2,8,1024]{0,3,1,2:T(8,128)}), f32[512,2,8,1024]{0,3,1,2:T(8,128)}, u32[]{:S(2)}, u32[]{:S(2)}) %all-to-all-start.2) | async-done | bytes 33554464 | tf_op jit(solution)/shard_map/all_to_all | solution.py:102
  927.1 7.1 all-to-all-start.6
  934.2 31.9 %copy.58 = f32[512,2,8,1024]{3,0,1,2:T(8,128)} copy(f32[512,2,8,1024]{0,3,1,2:T(8,128)} %all-to-all-done.2) | data formatting | bytes 67108864 | tf_op jit(solution)/shard_map/all_to_all | solution.py:102
  966.1 23.4 copy.59
  989.5 667.9 %all-to-all-done.6 = f32[512,2,4,2048]{3,2,1,0:T(4,128)} async-done(((f32[512,2,4,2048]{3,2,1,0:T(4,128)}), f32[512,2,4,2048]{3,2,1,0:T(4,128)}, u32[]{:S(2)}, u32[]{:S(2)}) %all-to-all-start.6) | async-done | bytes 33554464 | tf_op jit(solution)/shard_map/all_to_all | solution.py:78
  1657.4 9.7 all-to-all-start.3
  1667.1 37.9 %copy.66 = f32[512,2,4,2048]{0,3,1,2:T(8,128)} copy(f32[512,2,4,2048]{3,2,1,0:T(4,128)} %all-to-all-done.6) | data formatting | bytes 67108864 | tf_op jit(solution)/shard_map/all_to_all | solution.py:78
  1705.0 324.4 %all-to-all-done.3 = f32[8,4,128,2,1024]{4,2,3,0,1:T(8,128)} async-done(((f32[8,4,128,2,1024]{4,2,3,0,1:T(8,128)}), f32[8,4,128,2,1024]{4,2,3,0,1:T(8,128)}, u32[]{:S(2)}, u32[]{:S(2)}) %all-to-all-start.3) | async-done | bytes 33554464 | tf_op jit(solution)/shard_map/all_to_all | solution.py:108
  2029.4 9.7 all-to-all-start.7
  2040.0 8.0 scatter_custom_fusion.3
  2048.2 15.9 scatter_custom_fusion.1
  2064.1 23.5 copy.60
  2087.6 55.0 %copy.61 = f32[4096,2,1024]{2,1,0:T(2,128)} copy(f32[4096,2,1024]{2,0,1:T(8,128)} %bitcast.135) | data formatting | bytes 67108864 | tf_op jit(solution)/shard_map/reshape | solution.py:112
  2142.7 258.0 %all-to-all-done.7 = f32[512,2,4,2048]{0,3,1,2:T(8,128)} async-done(((f32[512,2,4,2048]{0,3,1,2:T(8,128)}), f32[512,2,4,2048]{0,3,1,2:T(8,128)}, u32[]{:S(2)}, u32[]{:S(2)}) %all-to-all-start.7) | async-done | bytes 33554464 | tf_op jit(solution)/shard_map/all_to_all | solution.py:77
  2400.6 31.8 %copy.67 = f32[512,2,4,2048]{3,0,2,1:T(8,128)} copy(f32[512,2,4,2048]{0,3,1,2:T(8,128)} %all-to-all-done.7) | data formatting | bytes 67108864 | tf_op jit(solution)/shard_map/all_to_all | solution.py:77
  2432.4 55.0 %copy.68 = f32[2048,2,2048]{2,1,0:T(2,128)} copy(f32[2048,2,2048]{2,0,1:T(8,128)} %bitcast.136) | data formatting | bytes 67108864 | tf_op jit(solution)/shard_map/reshape | solution.py:93
  2487.5 39.4 %gather_fusion.1 = f32[1024,2,2048]{2,1,0:T(2,128)} fusion(f32[2048,2,2048]{2,1,0:T(2,128)} %copy.68, s32[1024]{0:T(1024)S(1)} %fusion.22), kind=kCustom, calls=%fused_computation.5 | custom fusion | bytes 33558528 | tf_op jit(solution)/shard_map/jit(_take)/gather | solution.py:51
  2526.9 25.0 copy.69
  2551.9 54.2 %gather_fusion = f32[2048,2,1024]{2,1,0:T(2,128)} fusion(f32[4096,2,1024]{2,1,0:T(2,128)} %copy.61, s32[2048]{0:T(1024)S(1)} %fusion.19), kind=kCustom, calls=%fused_computation.4 | custom fusion | bytes 33562624 | tf_op jit(solution)/shard_map/jit(_take)/gather | solution.py:51
  2606.1 12.4 broadcast_select_fusion.3
  2618.5 4.1 copy-done.1
  2622.6 13.1 broadcast_select_fusion.2
  2635.7 19.2 fusion.31
  2655.6 17.8 fusion.1
  2673.4 16.7 fusion.3
  2690.2 13.8 fusion.2
  2704.0 13.6 subtract_bitcast_fusion.1
  2717.6 13.8 add_bitcast_fusion.1
  2733.9 51.4 %reduce-scatter.3.cloned.1.call-done = f32[256,2,512]{2,0,1:T(8,128)} async-done(((f32[1024,2,512]{2,0,1:T(8,128)}), f32[256,2,512]{2,0,1:T(8,128)}) %reduce-scatter.3.cloned.1.call-update) | async-done | bytes 1048592 | tf_op jit(solution)/shard_map/reduce_scatter | solution.py:130
  2787.7 52.7 %all-gather.5.cloned.1.call-done = f32[1024,2,512]{2,0,1:T(8,128)} async-done(((f32[256,2,512]{2,0,1:T(8,128)}), f32[1024,2,512]{2,0,1:T(8,128)}) %all-gather.5.cloned.1.call-update) | async-done | bytes 4194320 | tf_op jit(solution)/shard_map/all_gather | solution.py:134
  2840.4 17.2 fusion.6
  2857.7 16.0 fusion.7
  2873.7 15.1 add_bitcast_fusion
  2888.8 15.1 subtract_bitcast_fusion
  2904.0 4.2 pad_maximum_fusion
  2908.2 89.7 %reduce-scatter.5.cloned.1.call-done = f32[256,2,512]{2,0,1:T(8,128)} async-done(((f32[2048,2,512]{2,0,1:T(8,128)}), f32[256,2,512]{2,0,1:T(8,128)}) %reduce-scatter.5.cloned.1.call-update) | async-done | bytes 1048592 | tf_op jit(solution)/shard_map/reduce_scatter | solution.py:139
  (98 shorter events, 38.6 us)
Async XLA Ops:
  22.1 12.5 all-to-all-start.4
  35.1 10.7 all-to-all-start
  45.9 49.6 %all-to-all-start.5 = ((s32[512,1,4]{0,1,2:T(1,128)}), s32[512,1,4]{0,1,2:T(1,128)S(1)}, u32[]{:S(2)}, u32[]{:S(2)}) async-start(s32[512,1,4]{0,1,2:T(1,128)} %copy.63), calls=%async_computation.5 | async-start | bytes 16384 | tf_op jit(solution)/shard_map/all_to_all | solution.py:84
  95.5 0.6 copy-start.5
  96.1 100.0 %all-to-all-start.1 = ((s32[8,4,128]{2,0,1:T(8,128)}), s32[8,4,128]{2,0,1:T(8,128)S(1)}, u32[]{:S(2)}, u32[]{:S(2)}) async-start(s32[8,4,128]{2,0,1:T(8,128)} %bitcast.127), calls=%async_computation.1 | async-start | bytes 32768 | tf_op jit(solution)/shard_map/all_to_all | solution.py:109
  196.0 0.6 copy-start.3
  196.6 730.5 %all-to-all-start.2 = ((f32[512,2,8,1024]{0,3,1,2:T(8,128)}), f32[512,2,8,1024]{0,3,1,2:T(8,128)}, u32[]{:S(2)}, u32[]{:S(2)}) async-start(f32[512,2,8,1024]{0,3,1,2:T(8,128)} %copy.57), calls=%async_computation.2 | async-start | bytes 67108864 | tf_op jit(solution)/shard_map/all_to_all | solution.py:102
  927.1 730.3 %all-to-all-start.6 = ((f32[512,2,4,2048]{3,2,1,0:T(4,128)}), f32[512,2,4,2048]{3,2,1,0:T(4,128)}, u32[]{:S(2)}, u32[]{:S(2)}) async-start(f32[512,2,4,2048]{3,2,1,0:T(4,128)} %copy.65), calls=%async_computation.6 | async-start | bytes 67108864 | tf_op jit(solution)/shard_map/all_to_all | solution.py:78
  1657.4 372.0 %all-to-all-start.3 = ((f32[8,4,128,2,1024]{4,2,3,0,1:T(8,128)}), f32[8,4,128,2,1024]{4,2,3,0,1:T(8,128)}, u32[]{:S(2)}, u32[]{:S(2)}) async-start(f32[8,4,128,2,1024]{4,2,3,0,1:T(8,128)} %copy.59), calls=%async_computation.3 | async-start | bytes 67108864 | tf_op jit(solution)/shard_map/all_to_all | solution.py:108
  1705.0 334.9 %copy-start.7 = (s32[8,16]{1,0:T(8,128)S(1)}, s32[8,16]{1,0:T(8,128)}, u32[]{:S(2)}) copy-start(s32[8,16]{1,0:T(8,128)} %param.14) | copy-start | bytes 1540
  1705.0 335.0 %copy-start.6 = (s32[512,1,4]{0,1,2:T(1,128)S(1)}, s32[512,1,4]{0,1,2:T(1,128)}, u32[]{:S(2)}) copy-start(s32[512,1,4]{0,1,2:T(1,128)} %copy-done.5) | copy-start | bytes 24580
  1705.0 343.1 %copy-start.4 = (s32[8,4,128]{2,0,1:T(8,128)S(1)}, s32[8,4,128]{2,0,1:T(8,128)}, u32[]{:S(2)}) copy-start(s32[8,4,128]{2,0,1:T(8,128)} %copy-done.3) | copy-start | bytes 49156
  2029.4 371.3 %all-to-all-start.7 = ((f32[512,2,4,2048]{0,3,1,2:T(8,128)}), f32[512,2,4,2048]{0,3,1,2:T(8,128)}, u32[]{:S(2)}, u32[]{:S(2)}) async-start(f32[512,2,4,2048]{0,3,1,2:T(8,128)} %copy.66), calls=%async_computation.7 | async-start | bytes 67108864 | tf_op jit(solution)/shard_map/all_to_all | solution.py:77
  2039.1 634.3 %all-gather.3.cloned.1.call-start = ((), (), s32[]{:S(2)}) async-start(), calls=%async_computation.10 | async-start | bytes 9437184 | tf_op jit(solution)/shard_map/all_gather | solution.py:125
  2039.8 745.5 %reduce-scatter.3.cloned.1.call-start = ((), (), s32[]{:S(2)}) async-start(), calls=%async_computation.11 | async-start | bytes 5242880 | tf_op jit(solution)/shard_map/reduce_scatter | solution.py:130
  2606.1 16.5 copy-start.1
  2673.4 16.8 copy-start
  2673.4 16.8 copy-start.10
  2690.2 27.4 slice-start.2
  2703.9 13.6 slice-start.3
  2731.3 2.5 copy-start.8
  2731.3 2.5 copy-start.9
  2733.8 106.6 %all-gather.5.cloned.1.call-start = ((), (), s32[]{:S(2)}) async-start(), calls=%async_computation.12 | async-start | bytes 5242880 | tf_op jit(solution)/shard_map/all_gather | solution.py:134
  2787.7 210.2 %reduce-scatter.5.cloned.1.call-start = ((), (), s32[]{:S(2)}) async-start(), calls=%async_computation.13 | async-start | bytes 9437184 | tf_op jit(solution)/shard_map/reduce_scatter | solution.py:139
  2840.4 17.3 copy-start.2
  2840.4 33.3 %slice-start = ((s8[8388608]{0:T(1024)(128)(4,1)}), s8[4194304]{0:T(1024)(128)(4,1)S(1)}, s32[]{:S(2)}) async-start(s8[8388608]{0:T(1024)(128)(4,1)} %bitcast.137), calls=%async_computation.14 | async-start | bytes 8388608
  2857.7 16.0 slice-start.1
Sparse Core Ops, SparseCore 0:
  2041.5 81.8 all-gather.2
  2733.9 51.3 reduce-scatter.2
  2787.8 52.5 all-gather.4
  2908.3 89.5 reduce-scatter.4
where the time goes:
time: 3020 us; the launch traced here: 3000 us
  waiting for transfers between devices  2010 us (67%)
  local copies, waits for them, and re-layouts  696 us (23%)
  matrix products  121 us (4%)
  other arithmetic  106 us (4%)
  starting transfers between devices  53.3 us (2%)
    all_to_all x1, waiting for transfers between devices, local(): lax.all_to_all(outgoing, 'row', split_axis=0, concat_axis=0, tiled=True)  668 us
    all_to_all x1, waiting for transfers between devices, local(): lax.all_to_all(mirror_out, 'row', split_axis=2, concat_axis=0, tiled=True)  564 us
    all_to_all x1, waiting for transfers between devices, local(): lax.all_to_all(halfway, 'col', split_axis=1, concat_axis=0, tiled=True)  324 us
    all_to_all x1, waiting for transfers between devices, local(): lax.all_to_all(lax.all_to_all(outgoing, 'row', split_axis=0, concat_axis=...  258 us
    gather x3, local copies, waits for them, and re-layouts, place_rows(): return jnp.take(arrived, source, axis=0)  119 us
    select_n x2, local copies, waits for them, and re-layouts, pack_slots(): packed = jnp.take(traces, source, axis=0, mode='fill', fill_value=0.0)  97.5 us
    gather x2, local copies, waits for them, and re-layouts, pack_slots(): packed = jnp.take(traces, source, axis=0, mode='fill', fill_value=0.0)  91.8 us
    reduce_scatter x1, waiting for transfers between devices, local(): lax.psum_scatter(jnp.stack([image_re, image_im], axis=1), 'row', scatter_...  89.7 us
  transfers between devices with their start and end apart: 12, of which 8 were waited for; matrix products, arithmetic and copies ran while one was open for 26% of the time, Pallas kernels for 0%

commit v1 on v0

--- a/solution.py
+++ b/solution.py
@@ -2,6 +2,29 @@
 import jax.numpy as jnp
 from jax import lax
 from jax.sharding import PartitionSpec as P
+
+
+def in_blocks(x, dim, count):
+    shape = x.shape
+    blocks = x.reshape(*shape[:dim], count, shape[dim] // count, *shape[dim + 1 :])
+    return jnp.moveaxis(blocks, dim, 0)
+
+
+def joined_along(parts, dim):
+    lengths = list(parts.shape[1:])
+    lengths[dim] *= parts.shape[0]
+    return jnp.moveaxis(parts, 0, dim).reshape(lengths)
+
+
+def exchange_in_pairs(shard, axis, split_dim, concat_dim):
+    size, place = (lax.axis_size(axis), lax.axis_index(axis))
+    tiles = in_blocks(shard, split_dim, size)
+    outs = [tiles[place]]
+    for step in range(1, size):
+        sent = tiles[place ^ step]
+        outs.append(lax.ppermute(sent, axis, [(i, i ^ step) for i in range(size)]))
+    tiles = jnp.stack(outs)[place ^ jnp.arange(size)]
+    return joined_along(tiles, concat_dim)
 
 
 def high_dot(left, right):
@@ -74,12 +97,8 @@
     outgoing = packed.reshape(slot_total, 2, col_count, rcv_tile)
     label_copies = jnp.broadcast_to(packed_labels[:, None, None], (slot_total, 1, col_count))
     arrived, arrived_labels = (
-        lax.all_to_all(
-            lax.all_to_all(outgoing, "row", split_axis=0, concat_axis=0, tiled=True),
-            "col",
-            split_axis=2,
-            concat_axis=0,
-            tiled=True,
+        exchange_in_pairs(
+            lax.all_to_all(outgoing, "row", split_axis=0, concat_axis=0, tiled=True), "col", 2, 0
         ),
         lax.all_to_all(
             lax.all_to_all(label_copies, "row", split_axis=0, concat_axis=0, tiled=True),

time: 3020 us -> 2660 us (0.88)
  waiting for transfers between devices: 2010 us -> 1580 us
  other arithmetic: 106 us -> 179 us
    all_to_all x1 -> x0, waiting for transfers between devices: 258 us -> none  [local(): lax.all_to_all(lax.all_to_all(outgoing, 'row', split_axis=0, concat_axis=...]
    all_to_all x1, waiting for transfers between devices: 324 us -> 96.5 us  [local(): lax.all_to_all(halfway, 'col', split_axis=1, concat_axis=0, tiled=True)]
    all_to_all x1, waiting for transfers between devices: 564 us -> 702 us  [local(): lax.all_to_all(mirror_out, 'row', split_axis=2, concat_axis=0, tiled=True)]
    all_to_all x1, waiting for transfers between devices: 668 us -> 582 us  [local(): lax.all_to_all(outgoing, 'row', split_axis=0, concat_axis=0, tiled=True)]
    gather x0 -> x4, local copies, waits for them, and re-layouts: none -> 84.2 us  [exchange_in_pairs(): tiles = jnp.stack(outs)[place ^ jnp.arange(size)]]
    all_to_all x2 -> x0, local copies, waits for them, and re-layouts: 69.7 us -> none  [the longest x1 37.9 us: local(): lax.all_to_all(outgoing, 'row', split_axis=0, concat_axis=0, tiled=True)]
    dynamic_slice x0 -> x1, local copies, waits for them, and re-layouts: none -> 57.8 us  [exchange_in_pairs(): outs = [tiles[place]]]
    reshape x1 -> x0, local copies, waits for them, and re-layouts: 55 us -> none  [local(): arrived.reshape(-1, 2, rcv_tile)]
  transfers between devices with their start and end apart: 12 -> 14, of which waited for: 8 -> 7; matrix products, arithmetic and copies ran while one was open for 26% -> 32% of each run, Pallas kernels for 0% -> 0%
where the time goes in v1:
time: 2660 us; the launch traced here: 2640 us
  waiting for transfers between devices  1580 us (59%)
  local copies, waits for them, and re-layouts  701 us (26%)
  other arithmetic  179 us (7%)
  matrix products  121 us (5%)
  starting transfers between devices  46.6 us (2%)
    all_to_all x1, waiting for transfers between devices, local(): lax.all_to_all(mirror_out, 'row', split_axis=2, concat_axis=0, tiled=True)  702 us
    all_to_all x1, waiting for transfers between devices, local(): lax.all_to_all(outgoing, 'row', split_axis=0, concat_axis=0, tiled=True)  582 us
    gather x3, local copies, waits for them, and re-layouts, place_rows(): return jnp.take(arrived, source, axis=0)  119 us
    all_to_all x1, waiting for transfers between devices, local(): lax.all_to_all(halfway, 'col', split_axis=1, concat_axis=0, tiled=True)  96.5 us
    gather x2, local copies, waits for them, and re-layouts, pack_slots(): packed = jnp.take(traces, source, axis=0, mode='fill', fill_value=0.0)  91.7 us
    reduce_scatter x1, waiting for transfers between devices, local(): lax.psum_scatter(jnp.stack([image_re, image_im], axis=1), 'row', scatter_...  89.7 us
    gather x4, local copies, waits for them, and re-layouts, exchange_in_pairs(): tiles = jnp.stack(outs)[place ^ jnp.arange(size)]  84.2 us
    dot_general x4, matrix products, trans_dot(): lax.dot_general(left, right, (((0,), (0,)), ((), ())), precision=lax.Prec...  62.8 us
  transfers between devices with their start and end apart: 14, of which 7 were waited for; matrix products, arithmetic and copies ran while one was open for 32% of the time, Pallas kernels for 0%

profile of v1, /device:TPU:0, one launch (start us, length us, event | category | flops | bytes accessed | tf_op | source)
XLA Modules:
  0.0 2641.0 jit_solution(8462635906243502484)
XLA Ops:
  49.6 46.5 %gather_fusion.8 = f32[512,2,8192]{2,1,0:T(2,128)} fusion(f32[512,2,8192]{2,1,0:T(2,128)} %param.11, s32[1024]{0:T(1024)S(1)} %pad_clamp_fusion.1), kind=kCustom, calls=%fused_computation.3.clone | custom fusion | bytes 67110912 | tf_op jit(solution)/shard_map/jit(_take)/gather | solution.py:61
  100.6 24.2 broadcast_select_fusion
  124.8 45.8 %reshape.232 = f32[512,2,4,2048]{3,2,1,0:T(4,128)} reshape(f32[512,2,8192]{2,1,0:T(2,128)} %broadcast_select_fusion) | data formatting | bytes 67108864 | tf_op jit(solution)/shard_map/reshape | solution.py:97
  170.6 7.3 all-to-all-start.6
  177.9 45.2 %gather_fusion.6 = f32[512,2,8192]{2,1,0:T(2,128)} fusion(f32[512,2,8192]{2,1,0:T(2,128)} %param.11, s32[1024]{0:T(1024)S(1)} %pad_clamp_fusion.2), kind=kCustom, calls=%fused_computation.1.clone | custom fusion | bytes 67110912 | tf_op jit(solution)/shard_map/jit(_take)/gather | solution.py:61
  223.2 24.2 broadcast_select_fusion.1
  247.4 48.7 %copy.42 = f32[512,2,8192]{0,2,1:T(8,128)} copy(f32[512,2,8192]{2,1,0:T(2,128)} %broadcast_select_fusion.1) | data formatting | bytes 67108864 | tf_op jit(solution)/shard_map/jit(_take)/select_n | solution.py:61
  296.1 22.9 copy.43
  318.9 582.2 %all-to-all-done.6 = f32[512,2,4,2048]{3,2,1,0:T(4,128)} async-done(((f32[512,2,4,2048]{3,2,1,0:T(4,128)}), f32[512,2,4,2048]{3,2,1,0:T(4,128)}, u32[]{:S(2)}, u32[]{:S(2)}) %all-to-all-start.6) | async-done | bytes 33554464 | tf_op jit(solution)/shard_map/all_to_all | solution.py:101
  901.1 7.2 all-to-all-start.2
  908.4 57.8 %dynamic-slice_bitcast_fusion = (f32[1,512,2,1,2048]{4,3,2,1,0:T(1,128)}, f32[512,2,1,2048]{3,2,1,0:T(1,128)}, f32[512,2,1,2048]{3,2,1,0:T(1,128)}, f32[512,2,1,2048]{3,2,1,0:T(1,128)}) fusion(f32[512,2,4,2048]{3,2,1,0:T(4,128)} %all-to-all-done.6, s32[]{:T(128)S(6)} %select_n.163, s32[]{:T(128)S(6)} %select_n.166, s32[]{:T(128)S(6)} %select_n.165, ...), kind=kLoop, calls=%fused_computation.29 | loop fusion | bytes 67108880 | tf_op jit(solution)/shard_map/dynamic_slice | solution.py:22
  970.5 8.0 scatter_custom_fusion.3
  979.8 15.5 scatter_custom_fusion.1
  996.5 702.4 %all-to-all-done.2 = f32[512,2,8,1024]{0,3,1,2:T(8,128)} async-done(((f32[512,2,8,1024]{0,3,1,2:T(8,128)}), f32[512,2,8,1024]{0,3,1,2:T(8,128)}, u32[]{:S(2)}, u32[]{:S(2)}) %all-to-all-start.2) | async-done | bytes 33554464 | tf_op jit(solution)/shard_map/all_to_all | solution.py:121
  1698.9 31.9 %copy.44 = f32[512,2,8,1024]{3,0,1,2:T(8,128)} copy(f32[512,2,8,1024]{0,3,1,2:T(8,128)} %all-to-all-done.2) | data formatting | bytes 67108864 | tf_op jit(solution)/shard_map/all_to_all | solution.py:121
  1730.7 23.4 copy.45
  1754.1 9.7 all-to-all-start.3
  1764.1 9.1 pad_maximum_fusion.2
  1773.3 38.7 %pad_maximum_fusion = f32[4,512,2,1,2048]{4,3,2,1,0:T(1,128)} fusion(f32[1,512,2,1,2048]{4,3,2,1,0:T(1,128)} %bitcast.32, f32[1,512,2,1,2048]{4,3,2,1,0:T(1,128)} %bitcast.31, f32[1,512,2,1,2048]{4,3,2,1,0:T(1,128)} %bitcast.30, f32[1,512,2,1,2048]{4,3,2,1,0:T(1,128)} %get-tuple-element.10), kind=kLoop, calls=%fused_computation.13 | loop fusion | flops 25165824 | bytes 67108864 | tf_op jit(solution)/shard_map/stack | solution.py:26
  1811.9 20.3 fusion.32
  1832.2 8.5 copy.72
  1840.7 7.7 copy.70
  1848.3 13.8 gather_fusion.4
  1862.2 24.9 gather_fusion.3
  1887.1 18.7 copy.71
  1905.8 25.2 gather_fusion.2
  1931.0 22.7 pad_maximum_fusion.1
  1953.7 39.5 %gather_fusion.1 = f32[1024,2,2048]{2,1,0:T(2,128)} fusion(f32[2048,2,2048]{2,1,0:T(2,128)} %bitcast.153, s32[1024]{0:T(1024)S(1)} %copy-done.5), kind=kCustom, calls=%fused_computation.5 | custom fusion | bytes 33558528 | tf_op jit(solution)/shard_map/jit(_take)/gather | solution.py:74
  1993.2 25.0 copy.50
  2018.1 11.5 broadcast_select_fusion.3
  2029.6 96.5 %all-to-all-done.3 = f32[8,4,128,2,1024]{4,2,3,0,1:T(8,128)} async-done(((f32[8,4,128,2,1024]{4,2,3,0,1:T(8,128)}), f32[8,4,128,2,1024]{4,2,3,0,1:T(8,128)}, u32[]{:S(2)}, u32[]{:S(2)}) %all-to-all-start.3) | async-done | bytes 33554464 | tf_op jit(solution)/shard_map/all_to_all | solution.py:127
  2126.1 23.4 copy.46
  2149.4 55.0 %copy.47 = f32[4096,2,1024]{2,1,0:T(2,128)} copy(f32[4096,2,1024]{2,0,1:T(8,128)} %bitcast.148) | data formatting | bytes 67108864 | tf_op jit(solution)/shard_map/reshape | solution.py:131
  2204.5 54.2 %gather_fusion = f32[2048,2,1024]{2,1,0:T(2,128)} fusion(f32[4096,2,1024]{2,1,0:T(2,128)} %copy.47, s32[2048]{0:T(1024)S(1)} %copy-done.2), kind=kCustom, calls=%fused_computation.4 | custom fusion | bytes 33562624 | tf_op jit(solution)/shard_map/jit(_take)/gather | solution.py:74
  2258.7 14.0 broadcast_select_fusion.2
  2272.7 19.8 fusion.33
  2293.1 17.7 fusion.1
  2310.8 16.9 fusion.2
  2327.8 13.5 fusion.3
  2341.3 13.8 add_bitcast_fusion.1
  2355.1 13.5 subtract_bitcast_fusion.1
  2371.3 51.0 %reduce-scatter.3.cloned.1.call-done = f32[256,2,512]{2,0,1:T(8,128)} async-done(((f32[1024,2,512]{2,0,1:T(8,128)}), f32[256,2,512]{2,0,1:T(8,128)}) %reduce-scatter.3.cloned.1.call-update) | async-done | bytes 1048592 | tf_op jit(solution)/shard_map/reduce_scatter | solution.py:149
  2424.7 52.7 %all-gather.5.cloned.1.call-done = f32[1024,2,512]{2,0,1:T(8,128)} async-done(((f32[256,2,512]{2,0,1:T(8,128)}), f32[1024,2,512]{2,0,1:T(8,128)}) %all-gather.5.cloned.1.call-update) | async-done | bytes 4194320 | tf_op jit(solution)/shard_map/all_gather | solution.py:153
  2477.4 16.4 fusion.7
  2493.9 16.2 fusion.6
  2510.1 15.1 subtract_bitcast_fusion
  2525.2 15.1 add_bitcast_fusion
  2544.6 89.7 %reduce-scatter.5.cloned.1.call-done = f32[256,2,512]{2,0,1:T(8,128)} async-done(((f32[2048,2,512]{2,0,1:T(8,128)}), f32[256,2,512]{2,0,1:T(8,128)}) %reduce-scatter.5.cloned.1.call-update) | async-done | bytes 1048592 | tf_op jit(solution)/shard_map/reduce_scatter | solution.py:158
  (115 shorter events, 62.9 us)
Async XLA Ops:
  22.1 12.5 all-to-all-start.4
  35.2 10.7 all-to-all-start
  45.9 50.9 %all-to-all-start.5 = ((s32[512,1,4]{0,1,2:T(1,128)}), s32[512,1,4]{0,1,2:T(1,128)S(1)}, u32[]{:S(2)}, u32[]{:S(2)}) async-start(s32[512,1,4]{0,1,2:T(1,128)} %copy.49), calls=%async_computation.5 | async-start | bytes 16384 | tf_op jit(solution)/shard_map/all_to_all | solution.py:103
  96.7 0.6 copy-start.3
  97.3 73.3 %all-to-all-start.1 = ((s32[8,4,128]{2,0,1:T(8,128)}), s32[8,4,128]{2,0,1:T(8,128)S(1)}, u32[]{:S(2)}, u32[]{:S(2)}) async-start(s32[8,4,128]{2,0,1:T(8,128)} %bitcast.141), calls=%async_computation.1 | async-start | bytes 32768 | tf_op jit(solution)/shard_map/all_to_all | solution.py:128
  170.6 730.5 %all-to-all-start.6 = ((f32[512,2,4,2048]{3,2,1,0:T(4,128)}), f32[512,2,4,2048]{3,2,1,0:T(4,128)}, u32[]{:S(2)}, u32[]{:S(2)}) async-start(f32[512,2,4,2048]{3,2,1,0:T(4,128)} %reshape.232), calls=%async_computation.6 | async-start | bytes 67108864 | tf_op jit(solution)/shard_map/all_to_all | solution.py:101
  901.1 797.8 %all-to-all-start.2 = ((f32[512,2,8,1024]{0,3,1,2:T(8,128)}), f32[512,2,8,1024]{0,3,1,2:T(8,128)}, u32[]{:S(2)}, u32[]{:S(2)}) async-start(f32[512,2,8,1024]{0,3,1,2:T(8,128)} %copy.43), calls=%async_computation.2 | async-start | bytes 67108864 | tf_op jit(solution)/shard_map/all_to_all | solution.py:121
  908.3 1402.5 %all-gather.3.cloned.1.call-start = ((), (), s32[]{:S(2)}) async-start(), calls=%async_computation.9 | async-start | bytes 9437184 | tf_op jit(solution)/shard_map/all_gather | solution.py:144
  908.4 61.4 %copy-start.9 = (s32[8,16]{1,0:T(8,128)S(1)}, s32[8,16]{1,0:T(8,128)}, u32[]{:S(2)}) copy-start(s32[8,16]{1,0:T(8,128)} %param.14) | copy-start | bytes 1540
  908.4 62.1 %copy-start.4 = (s32[512,1,4]{0,1,2:T(1,128)S(1)}, s32[512,1,4]{0,1,2:T(1,128)}, u32[]{:S(2)}) copy-start(s32[512,1,4]{0,1,2:T(1,128)} %copy-done.3) | copy-start | bytes 24580
  966.2 797.9 %collective-permute-start.2 = (f32[512,2,1,2048]{3,2,1,0:T(1,128)}, f32[512,2,1,2048]{3,2,1,0:T(1,128)}, u32[]{:S(2)}, u32[]{:S(2)}) collective-permute-start(f32[512,2,1,2048]{3,2,1,0:T(1,128)} %get-tuple-element.11), channel_id=1, source_target_pairs={{0,3},{1,2},{2,1},{3,0},{4,7},{5,6},{6,5},{7,4},{8,11},{9,10},{10,... | collective-permute-start | bytes 25165832 | tf_op jit(solution)/shard_map/ppermute | solution.py:25
  969.1 795.0 %collective-permute-start.1 = (f32[512,2,1,2048]{3,2,1,0:T(1,128)}, f32[512,2,1,2048]{3,2,1,0:T(1,128)}, u32[]{:S(2)}, u32[]{:S(2)}) collective-permute-start(f32[512,2,1,2048]{3,2,1,0:T(1,128)} %get-tuple-element.12), channel_id=1, source_target_pairs={{0,2},{1,3},{2,0},{3,1},{4,6},{5,7},{6,4},{7,5},{8,10},{9,11},{10,... | collective-permute-start | bytes 25165832 | tf_op jit(solution)/shard_map/ppermute | solution.py:25
  969.7 794.4 %collective-permute-start = (f32[512,2,1,2048]{3,2,1,0:T(1,128)}, f32[512,2,1,2048]{3,2,1,0:T(1,128)}, u32[]{:S(2)}, u32[]{:S(2)}) collective-permute-start(f32[512,2,1,2048]{3,2,1,0:T(1,128)} %get-tuple-element.13), channel_id=1, source_target_pairs={{0,1},{1,0},{2,3},{3,2},{4,5},{5,4},{6,7},{7,6},{8,9},{9,8},{10,11... | collective-permute-start | bytes 25165832 | tf_op jit(solution)/shard_map/ppermute | solution.py:25
  1754.1 372.0 %all-to-all-start.3 = ((f32[8,4,128,2,1024]{4,2,3,0,1:T(8,128)}), f32[8,4,128,2,1024]{4,2,3,0,1:T(8,128)}, u32[]{:S(2)}, u32[]{:S(2)}) async-start(f32[8,4,128,2,1024]{4,2,3,0,1:T(8,128)} %copy.45), calls=%async_computation.3 | async-start | bytes 67108864 | tf_op jit(solution)/shard_map/all_to_all | solution.py:127
  1763.8 658.5 %reduce-scatter.3.cloned.1.call-start = ((), (), s32[]{:S(2)}) async-start(), calls=%async_computation.10 | async-start | bytes 5242880 | tf_op jit(solution)/shard_map/reduce_scatter | solution.py:149
  1931.0 22.7 copy-start.5
  1993.2 25.0 copy-start.8
  2149.4 55.0 %copy-start.2 = (s32[2048]{0:T(1024)S(1)}, s32[2048]{0:T(1024)}, u32[]{:S(2)}) copy-start(s32[2048]{0:T(1024)} %fusion.19) | copy-start | bytes 24580
  2204.5 54.2 %copy-start.6 = (pred[2048]{0:T(1024)(128)(4,1)S(1)}, pred[2048]{0:T(1024)(128)(4,1)}, u32[]{:S(2)}) copy-start(pred[2048]{0:T(1024)(128)(4,1)} %compare_and_fusion) | copy-start | bytes 6148
  2272.7 19.8 copy-start.7
  2310.8 16.9 copy-start
  2310.8 16.9 copy-start.12
  2327.8 27.3 %slice-start = ((s8[8388608]{0:T(1024)(128)(4,1)}), s8[4194304]{0:T(1024)(128)(4,1)S(1)}, s32[]{:S(2)}) async-start(s8[8388608]{0:T(1024)(128)(4,1)} %bitcast.149), calls=%async_computation.13 | async-start | bytes 8388608
  2341.3 13.8 slice-start.1
  2368.7 2.5 copy-start.10
  2368.7 2.5 copy-start.11
  2371.1 106.3 %all-gather.5.cloned.1.call-start = ((), (), s32[]{:S(2)}) async-start(), calls=%async_computation.11 | async-start | bytes 5242880 | tf_op jit(solution)/shard_map/all_gather | solution.py:153
  2424.7 209.6 %reduce-scatter.5.cloned.1.call-start = ((), (), s32[]{:S(2)}) async-start(), calls=%async_computation.12 | async-start | bytes 9437184 | tf_op jit(solution)/shard_map/reduce_scatter | solution.py:158
  2477.4 16.4 copy-start.1
  2477.4 32.7 %slice-start.2 = ((s8[8388608]{0:T(1024)(128)(4,1)}), s8[4194304]{0:T(1024)(128)(4,1)S(1)}, s32[]{:S(2)}) async-start(s8[8388608]{0:T(1024)(128)(4,1)} %bitcast.151), calls=%async_computation.15 | async-start | bytes 8388608
  2493.9 16.2 slice-start.3
Sparse Core Ops, SparseCore 0:
  969.9 175.7 all-gather.2
  2371.3 51.0 reduce-scatter.2
  2424.8 52.5 all-gather.4
  2544.7 89.5 reduce-scatter.4
